TPU v7x, 32 devices: a whole 2x2x4 slice. The times are simulated.
32 devices in a mesh: wide: 8 (over y, x, core), quad: 4 (over z).
Axes of the slice: x: 2, y: 2, z: 4, core: 2. Of those that a mesh axis runs over, the one named last changes fastest.
Arguments:
- basis: float32 [16, 2097152], P(None, ('wide', 'quad')), may hold values from -6 to 6
- target: float32 [2097152], P(('wide', 'quad')), may hold values from -6 to 6
- sign_bits: int32 [2097152], P(('wide', 'quad')), may hold values from 0 to 1
- samples: int32 [8192], replicated, may hold values from 0 to 2097151
- owners: int32 [8192], replicated, may hold values from 0 to 7
Outputs:
- sketch: float32 [8192, 17], P(('wide', 'quad'))
- gram: float32 [8, 16, 17], P('quad')
Inputs may be any that keep to these rules, and one draw needn't show every extreme that they name: `samples`: sampled scenarios may repeat.
All inputs are finite; a program needn't handle non-finite values.
Results may differ from a plain program's by a relative error of at most 0.0003.
Values sent between devices are 32-bit elements; how exact they have to be, the bound alone decides.
A program may use at most 128 MiB of HBM per device.

v0:
```python
import math
import jax
import jax.numpy as jnp
from jax import lax
from jax.sharding import PartitionSpec as P

GROUPS = 8


def parity_sign(first, second, nbits):
    count = jnp.zeros_like(first)
    for bit in range(nbits):
        count = count + ((first & second) >> bit) & 1
    return (1 - 2 * (count & 1)).astype(jnp.float32)


def walsh_table(order):
    nbits = order.bit_length() - 1
    line = jnp.arange(order, dtype=jnp.int32)
    return parity_sign(line[:, None], line[None, :], nbits)


def shards(basis, target, sign_bits, samples, owners):
    rows = basis.shape[1]
    block = math.isqrt(rows)
    n_wide = lax.axis_size("wide")
    n_quad = lax.axis_size("quad")
    devices = n_wide * n_quad
    my_wide = lax.axis_index("wide")
    my_quad = lax.axis_index("quad")
    my_device = my_wide * n_quad + my_quad
    total_samples = samples.shape[0]
    per_dev = total_samples // devices
    scale = 1.0 / math.sqrt(rows * devices)
    flip = (1 - 2 * sign_bits).astype(jnp.float32)
    signed = jnp.concatenate([basis, target[None, :]], axis=0) * flip[None, :]
    width = signed.shape[0]
    table = walsh_table(block)
    cube = signed.reshape(width, block, block)
    cube = jnp.einsum("kab,ac->kcb", cube, table, precision=lax.Precision.HIGHEST)
    cube = jnp.einsum("kcb,bd->kcd", cube, table, precision=lax.Precision.HIGHEST)
    local = cube.reshape(width, rows)
    quarter = total_samples // n_quad
    quad_bits = n_quad.bit_length() - 1
    wide_bits = n_wide.bit_length() - 1
    line = jnp.arange(total_samples, dtype=jnp.int32)
    inner = line // quarter
    rest = line % quarter
    slots = (rest // per_dev * n_quad + inner) * per_dev + rest % per_dev
    number = samples[slots]
    values = jnp.take(local, number % rows, axis=1)
    source, values = (number // rows, values)
    sign = parity_sign(source % n_quad, jnp.full_like(source, my_quad), quad_bits)
    shared = lax.psum_scatter(values * sign[None, :], "quad", scatter_dimension=1, tiled=True)
    second = jnp.arange(quarter, dtype=jnp.int32)
    mine = (second // per_dev * n_quad + my_quad) * per_dev + second % per_dev
    outer = samples[mine] // rows // n_quad
    wide_sign = parity_sign(outer, jnp.full_like(outer, my_wide), wide_bits)
    columns = lax.psum_scatter(
        shared * (scale * wide_sign)[None, :], "wide", scatter_dimension=1, tiled=True
    )
    sketch = columns.T
    own_groups = lax.dynamic_slice_in_dim(owners, my_device * per_dev, per_dev, 0)
    onehot = (own_groups[:, None] == jnp.arange(GROUPS, dtype=jnp.int32)[None, :]).astype(
        jnp.float32
    )
    partial_gram = jnp.einsum(
        "rg,ri,rj->gij", onehot, sketch[:, : width - 1], sketch, precision=lax.Precision.HIGHEST
    )
    partial_gram = partial_gram * (GROUPS / total_samples)
    owned = GROUPS // n_quad
    summed = lax.psum(partial_gram, ("wide", "quad"))
    gram = lax.dynamic_slice_in_dim(summed, my_quad * owned, owned, 0)
    return (sketch, gram)


def solution(mesh):
    placed = (P(None, ("wide", "quad")), P(("wide", "quad")), P(("wide", "quad")), P(), P())
    return jax.shard_map(
        shards,
        mesh=mesh,
        in_specs=placed,
        out_specs=(P(("wide", "quad"), None), P("quad", None, None)),
        check_vma=False,
    )
```

profile of v0, /device:TPU:0, one launch (start us, length us, event | category | flops | bytes accessed | tf_op | source)
XLA Modules:
  0.0 308.2 jit_solution(10460242113116470487)
XLA Ops:
  7.2 0.0 copy-start
  7.2 0.0 reduce-scatter.3.cloned.1.call-start
  7.2 0.1 compare_select_fusion.1
  7.3 0.0 copy-start.1
  7.4 1.1 concatenate.9
  8.4 5.4 %copy.20 = f32[2,8,256,256]{3,2,1,0:T(8,128)} copy(f32[2,8,256,256]{3,1,2,0:T(8,128)} %bitcast.26) | data formatting | bytes 8388608
  13.8 0.0 copy-done.1
  13.8 0.1 mul.137
  13.9 6.7 %fusion = f32[256,17,256]{2,0,1:T(8,128)S(1)} fusion(f32[1,256,256]{2,1,0:T(8,128)S(1)} %concatenate.9, f32[16,256,256]{2,1,0:T(8,128)} %bitcast.25, f32[256,256]{1,0:T(8,128)S(1)} %mul.137), kind=kOutput, calls=%fused_computation.4 | convolution fusion | flops 3426615296 | bytes 9175040 | tf_op jit(solution)/shard_map/kab,ac->kcb/dot_general | solution.py:40
  20.6 5.7 %fusion.3 = f32[17,256,256]{2,1,0:T(8,128)} fusion(f32[256,17,256]{2,0,1:T(8,128)S(1)} %fusion), kind=kOutput, calls=%fused_computation.7 | convolution fusion | flops 3424387072 | bytes 8912896 | tf_op jit(solution)/shard_map/kcb,bd->kcd/dot_general | solution.py:41
  26.3 18.0 %copy.18 = f32[17,256,256]{0,2,1:T(8,128)} copy(f32[17,256,256]{2,1,0:T(8,128)} %fusion.3) | data formatting | bytes 8912896 | tf_op jit(solution)/shard_map/reshape | solution.py:42
  44.3 0.0 copy-done
  44.3 45.5 %gather_fusion = s32[8192]{0:T(1024)S(1)} fusion(s32[8192]{0:T(1024)S(1)} %copy-done, s32[8192]{0:T(1024)S(1)} %broadcast_clamp_fusion.1), kind=kCustom, calls=%fused_computation | custom fusion | bytes 98304 | tf_op jit(solution)/shard_map/gather | solution.py:50
  89.9 0.1 compare_select_fusion
  90.0 0.1 subtract_convert_fusion.1
  90.1 38.2 %gather_fusion.1 = f32[8192,17]{1,0:T(8,128)} fusion(f32[17,65536]{0,1:T(8,128)} %bitcast.24, s32[8192]{0:T(1024)S(1)} %broadcast_clamp_fusion), kind=kCustom, calls=%fused_computation.1 | custom fusion | bytes 1146880 | tf_op jit(solution)/shard_map/jit(_take)/gather | solution.py:51
  128.3 9.7 %multiply_bitcast_fusion = f32[17,8192]{0,1:T(8,128)} fusion(f32[8192,17]{1,0:T(8,128)} %gather_fusion.1, f32[8192]{0:T(1024)S(1)} %subtract_convert_fusion.1, pred[8192]{0:T(1024)(128)(4,1)S(1)} %compare_and_fusion), kind=kLoop, calls=%fused_computation.9 | loop fusion | flops 278528 | bytes 1155072 | tf_op jit(solution)/shard_map/mul | solution.py:54
  138.0 0.0 reduce-scatter.3.cloned.1.call-update
  138.0 0.0 reduce-scatter.5.cloned.1.call-start
  138.1 11.8 %gather_fusion.2 = s32[2048]{0:T(1024)S(1)} fusion(s32[8192]{0:T(1024)S(1)} %copy-done, s32[2048]{0:T(1024)S(1)} %broadcast_clamp_fusion.2), kind=kCustom, calls=%fused_computation.2 | custom fusion | bytes 24576 | tf_op jit(solution)/shard_map/gather | solution.py:57
  149.9 0.8 dynamic_slice.6
  150.7 67.0 %reduce-scatter.3.cloned.1.call-done = f32[17,2048]{0,1:T(8,128)} async-done(((f32[17,8192]{0,1:T(8,128)}), f32[17,2048]{0,1:T(8,128)}) %reduce-scatter.3.cloned.1.call-update) | async-done | bytes 139280 | tf_op jit(solution)/shard_map/reduce_scatter | solution.py:54
  217.7 2.6 broadcast_multiply_fusion
  220.3 0.0 reduce-scatter.5.cloned.1.call-update
  220.3 37.1 %reduce-scatter.5.cloned.1.call-done = f32[17,256]{0,1:T(8,128)} async-done(((f32[17,2048]{0,1:T(8,128)}), f32[17,256]{0,1:T(8,128)}) %reduce-scatter.5.cloned.1.call-update) | async-done | bytes 17424 | tf_op jit(solution)/shard_map/reduce_scatter | solution.py:59
  257.4 1.6 copy.15
  259.0 1.0 copy.13
  260.0 1.2 fusion.6
  261.1 39.6 %psum.7 = f32[8,16,17]{2,0,1:T(8,128)S(1)} all-reduce(f32[8,16,17]{2,0,1:T(8,128)S(1)} %fusion.6), channel_id=1, replica_groups=mesh['wide'=8,'quad'=4] {'wide','quad'}, use_global_device_ids=true, to_apply=%region_2.3 | all-reduce | flops 2176 | bytes 17408 | tf_op jit(solution)/shard_map/psum | solution.py:72
  300.8 0.6 copy.16
  (9 shorter events, 0.2 us)
Async XLA Ops:
  7.2 37.1 %copy-start = (s32[8192]{0:T(1024)S(1)}, s32[8192]{0:T(1024)}, u32[]{:S(2)}) copy-start(s32[8192]{0:T(1024)} %param.8) | copy-start | bytes 98308
  7.2 210.5 %reduce-scatter.3.cloned.1.call-start = ((), (), s32[]{:S(2)}) async-start(), calls=%async_computation.2 | async-start | bytes 5242880 | tf_op jit(solution)/shard_map/reduce_scatter | solution.py:54
  7.3 6.4 %copy-start.1 = (s32[65536]{0:T(1024)S(1)}, s32[65536]{0:T(1024)}, u32[]{:S(2)}) copy-start(s32[65536]{0:T(1024)} %param.7) | copy-start | bytes 786436
  138.0 119.4 %reduce-scatter.5.cloned.1.call-start = ((), (), s32[]{:S(2)}) async-start(), calls=%async_computation.3 | async-start | bytes 1179648 | tf_op jit(solution)/shard_map/reduce_scatter | solution.py:59
Sparse Core Ops, SparseCore 0:
  138.2 79.5 reduce-scatter.2
  220.9 36.4 reduce-scatter.4
where the time goes:
time: 309 us; the launch traced here: 308 us
  local copies, waits for them, and re-layouts  124 us (40%)
  waiting for transfers between devices  104 us (34%)
  blocking collectives  39.6 us (13%)
  between operations  14.2 us (5%)
  matrix products  13.6 us (4%)
  other arithmetic  12.7 us (4%)
    reduce_scatter x1, waiting for transfers between devices, shards(): lax.psum_scatter(values * sign[None, :], 'quad', scatter_dimension=1, til...  67 us
    gather x1, local copies, waits for them, and re-layouts, shards(): number = samples[slots]  45.5 us
    psum x1, blocking collectives, shards(): summed = lax.psum(partial_gram, ('wide', 'quad'))  39.6 us
    gather x1, local copies, waits for them, and re-layouts, shards(): values = jnp.take(local, number % rows, axis=1)  38.2 us
    reduce_scatter x1, waiting for transfers between devices, shards(): lax.psum_scatter(shared * (scale * wide_sign)[None, :], 'wide', scatter_d...  37.1 us
    reshape x1, local copies, waits for them, and re-layouts, shards(): local = cube.reshape(width, rows)  18 us
    gather x1, local copies, waits for them, and re-layouts, shards(): outer = samples[mine] // rows // n_quad  11.8 us
    mul x1, other arithmetic, shards(): values * sign[None, :]  9.67 us
  transfers between devices with their start and end apart: 2, of which 2 were waited for; matrix products, arithmetic and copies ran while one was open for 4% of the time, Pallas kernels for 0%

commit v1 on v0

--- a/solution.py
+++ b/solution.py
@@ -5,6 +5,11 @@
 from jax.sharding import PartitionSpec as P
 
 GROUPS = 8
+
+
+def add_all(value, name):
+    shards = lax.all_gather(value, name)
+    return jnp.sum(shards, axis=0)
 
 
 def parity_sign(first, second, nbits):
@@ -69,7 +74,7 @@
     )
     partial_gram = partial_gram * (GROUPS / total_samples)
     owned = GROUPS // n_quad
-    summed = lax.psum(partial_gram, ("wide", "quad"))
+    summed = add_all(partial_gram, ("wide", "quad"))
     gram = lax.dynamic_slice_in_dim(summed, my_quad * owned, owned, 0)
     return (sketch, gram)
 

time: 309 us -> 357 us (1.16)
  blocking collectives: 39.6 us -> 87.7 us
    all_gather x0 -> x1, blocking collectives: none -> 87.7 us  [add_all(): shards = lax.all_gather(value, name)]
    psum x1 -> x0, blocking collectives: 39.6 us -> none  [shards(): summed = lax.psum(partial_gram, ('wide', 'quad'))]
where the time goes in v1:
time: 357 us
  local copies, waits for them, and re-layouts  124 us (35%)
  waiting for transfers between devices  104 us (29%)
  blocking collectives  87.7 us (25%)
  between operations  14.2 us (4%)
  matrix products  13.6 us (4%)
  other arithmetic  12.8 us (4%)
    all_gather x1, blocking collectives, add_all(): shards = lax.all_gather(value, name)  87.7 us
    reduce_scatter x1, waiting for transfers between devices, shards(): lax.psum_scatter(values * sign[None, :], 'quad', scatter_dimension=1, til...  67 us
    gather x1, local copies, waits for them, and re-layouts, shards(): number = samples[slots]  45.5 us
    gather x1, local copies, waits for them, and re-layouts, shards(): values = jnp.take(local, number % rows, axis=1)  38.2 us
    reduce_scatter x1, waiting for transfers between devices, shards(): lax.psum_scatter(shared * (scale * wide_sign)[None, :], 'wide', scatter_d...  37.1 us
    reshape x1, local copies, waits for them, and re-layouts, shards(): local = cube.reshape(width, rows)  18 us
    gather x1, local copies, waits for them, and re-layouts, shards(): outer = samples[mine] // rows // n_quad  11.8 us
    mul x1, other arithmetic, shards(): values * sign[None, :]  9.67 us
  transfers between devices with their start and end apart: 2, of which 2 were waited for; matrix products, arithmetic and copies ran while one was open for 4% of the time, Pallas kernels for 0%

profile of v1, /device:TPU:0, one launch (start us, length us, event | category | flops | bytes accessed | tf_op | source)
XLA Modules:
  0.0 356.5 jit_solution(13810625368041413566)
XLA Ops:
  7.2 0.0 copy-start
  7.2 0.0 reduce-scatter.3.cloned.1.call-start
  7.2 0.1 compare_select_fusion.1
  7.3 0.0 copy-start.1
  7.4 1.1 concatenate.9
  8.4 5.4 %copy.26 = f32[2,8,256,256]{3,2,1,0:T(8,128)} copy(f32[2,8,256,256]{3,1,2,0:T(8,128)} %bitcast.29) | data formatting | bytes 8388608
  13.8 0.0 copy-done.1
  13.8 0.1 mul.137
  13.9 6.7 %fusion = f32[256,17,256]{2,0,1:T(8,128)S(1)} fusion(f32[1,256,256]{2,1,0:T(8,128)S(1)} %concatenate.9, f32[16,256,256]{2,1,0:T(8,128)} %bitcast.28, f32[256,256]{1,0:T(8,128)S(1)} %mul.137), kind=kOutput, calls=%fused_computation.4 | convolution fusion | flops 3426615296 | bytes 9175040 | tf_op jit(solution)/shard_map/kab,ac->kcb/dot_general | solution.py:45
  20.6 5.7 %fusion.3 = f32[17,256,256]{2,1,0:T(8,128)} fusion(f32[256,17,256]{2,0,1:T(8,128)S(1)} %fusion), kind=kOutput, calls=%fused_computation.7 | convolution fusion | flops 3424387072 | bytes 8912896 | tf_op jit(solution)/shard_map/kcb,bd->kcd/dot_general | solution.py:46
  26.3 18.0 %copy.24 = f32[17,256,256]{0,2,1:T(8,128)} copy(f32[17,256,256]{2,1,0:T(8,128)} %fusion.3) | data formatting | bytes 8912896 | tf_op jit(solution)/shard_map/reshape | solution.py:47
  44.3 0.0 copy-done
  44.3 45.5 %gather_fusion = s32[8192]{0:T(1024)S(1)} fusion(s32[8192]{0:T(1024)S(1)} %copy-done, s32[8192]{0:T(1024)S(1)} %broadcast_clamp_fusion.1), kind=kCustom, calls=%fused_computation | custom fusion | bytes 98304 | tf_op jit(solution)/shard_map/gather | solution.py:55
  89.9 0.1 compare_select_fusion
  90.0 0.1 subtract_convert_fusion.1
  90.1 38.2 %gather_fusion.1 = f32[8192,17]{1,0:T(8,128)} fusion(f32[17,65536]{0,1:T(8,128)} %bitcast.27, s32[8192]{0:T(1024)S(1)} %broadcast_clamp_fusion), kind=kCustom, calls=%fused_computation.1 | custom fusion | bytes 1146880 | tf_op jit(solution)/shard_map/jit(_take)/gather | solution.py:56
  128.3 9.7 %multiply_bitcast_fusion = f32[17,8192]{0,1:T(8,128)} fusion(f32[8192,17]{1,0:T(8,128)} %gather_fusion.1, f32[8192]{0:T(1024)S(1)} %subtract_convert_fusion.1, pred[8192]{0:T(1024)(128)(4,1)S(1)} %compare_and_fusion), kind=kLoop, calls=%fused_computation.9 | loop fusion | flops 278528 | bytes 1155072 | tf_op jit(solution)/shard_map/mul | solution.py:59
  138.0 0.0 reduce-scatter.3.cloned.1.call-update
  138.0 0.0 reduce-scatter.5.cloned.1.call-start
  138.1 11.8 %gather_fusion.2 = s32[2048]{0:T(1024)S(1)} fusion(s32[8192]{0:T(1024)S(1)} %copy-done, s32[2048]{0:T(1024)S(1)} %broadcast_clamp_fusion.2), kind=kCustom, calls=%fused_computation.2 | custom fusion | bytes 24576 | tf_op jit(solution)/shard_map/gather | solution.py:62
  149.9 0.8 dynamic_slice.6
  150.7 67.0 %reduce-scatter.3.cloned.1.call-done = f32[17,2048]{0,1:T(8,128)} async-done(((f32[17,8192]{0,1:T(8,128)}), f32[17,2048]{0,1:T(8,128)}) %reduce-scatter.3.cloned.1.call-update) | async-done | bytes 139280 | tf_op jit(solution)/shard_map/reduce_scatter | solution.py:59
  217.7 2.6 broadcast_multiply_fusion
  220.3 0.0 reduce-scatter.5.cloned.1.call-update
  220.3 37.1 %reduce-scatter.5.cloned.1.call-done = f32[17,256]{0,1:T(8,128)} async-done(((f32[17,2048]{0,1:T(8,128)}), f32[17,256]{0,1:T(8,128)}) %reduce-scatter.5.cloned.1.call-update) | async-done | bytes 17424 | tf_op jit(solution)/shard_map/reduce_scatter | solution.py:64
  257.4 1.6 copy.19
  259.0 1.0 copy.17
  260.0 1.2 fusion.6
  261.1 87.7 %all-gather = f32[256,16,17]{2,0,1:T(8,128)S(1)} all-gather(f32[8,16,17]{2,0,1:T(8,128)S(1)} %fusion.6), channel_id=2, replica_groups=mesh['wide'=8,'quad'=4] {'wide','quad'}, dimensions={0}, use_global_device_ids=true | all-gather | bytes 287232 | tf_op jit(solution)/shard_map/all_gather | solution.py:11
  348.9 0.1 bitcast_reduce_fusion
  349.1 0.6 copy.20
  (9 shorter events, 0.1 us)
Async XLA Ops:
  7.2 37.1 %copy-start = (s32[8192]{0:T(1024)S(1)}, s32[8192]{0:T(1024)}, u32[]{:S(2)}) copy-start(s32[8192]{0:T(1024)} %param.8) | copy-start | bytes 98308
  7.2 210.5 %reduce-scatter.3.cloned.1.call-start = ((), (), s32[]{:S(2)}) async-start(), calls=%async_computation.2 | async-start | bytes 5242880 | tf_op jit(solution)/shard_map/reduce_scatter | solution.py:59
  7.3 6.4 %copy-start.1 = (s32[65536]{0:T(1024)S(1)}, s32[65536]{0:T(1024)}, u32[]{:S(2)}) copy-start(s32[65536]{0:T(1024)} %param.7) | copy-start | bytes 786436
  138.0 119.4 %reduce-scatter.5.cloned.1.call-start = ((), (), s32[]{:S(2)}) async-start(), calls=%async_computation.3 | async-start | bytes 1179648 | tf_op jit(solution)/shard_map/reduce_scatter | solution.py:64
Sparse Core Ops, SparseCore 0:
  138.2 79.5 reduce-scatter.2
  220.9 36.4 reduce-scatter.4
